TPU v7x, 32 devices: a whole 2x2x4 slice. The times are simulated.
32 devices in a mesh: seq: 16 (over z, y, x), head: 2 (over core).
Axes of the slice: x: 2, y: 2, z: 4, core: 2. Of those that a mesh axis runs over, the one named last changes fastest.
Arguments:
- query_raw: bfloat16 [2048, 2048], P('seq', 'head'), may hold values from -6 to 6
- key_raw: bfloat16 [2048, 2048], P('seq', 'head'), may hold values from -6 to 6
- value_raw: bfloat16 [2048, 2048], P('seq', 'head'), may hold values from -6 to 6
- gate_raw: float32 [2048, 2048], P('seq', 'head')
- beta_raw: float32 [2048, 16], P('seq', 'head'), may hold values from -8.5 to 3.5
- conv_weight: float32 [3, 4, 2048], P(None, None, 'head'), may hold values from -3 to 3
- decay_log: float32 [2048], P('head')
- grad_out: bfloat16 [2048, 2048], P('seq', 'head'), may hold values from -6 to 6
Outputs:
- query_grad: bfloat16 [2048, 2048], P('seq', 'head')
- key_grad: bfloat16 [2048, 2048], P('seq', 'head')
- value_grad: bfloat16 [2048, 2048], P('seq', 'head')
- gate_grad: float32 [2048, 2048], P('seq', 'head')
- beta_grad: float32 [2048, 16], P('seq', 'head')
- conv_grad: float32 [3, 4, 2048], P(None, None, 'head')
- decay_grad: float32 [2048], P('head')
All inputs are finite; a program needn't handle non-finite values.
Results may differ from a plain program's by a relative error of at most 0.0018.
Values may be sent and summed in bfloat16 or wider, within the bound.
A program may use at most 128 MiB of HBM per device.

v0:
```python
import functools
import math

import jax
import jax.numpy as jnp
from jax import lax
from jax.experimental import pallas as pl
from jax.experimental.pallas import tpu as pltpu
from jax.sharding import PartitionSpec as P

F32 = jnp.float32
BF16 = jnp.bfloat16
EPS = 1e-06
PAD = 8
RED = 16
GROUP = 4
GROUP_MAPS = 4
LINK = F32
TEAM = 4
VMEM_LIMIT = 60 * 1024 * 1024


def split(x):
    hi = x.astype(BF16)
    return hi, (x - hi.astype(F32)).astype(BF16)


def mm(a, b, ta=False, tb=False):
    ah, al = split(a)
    bh, bl = split(b)
    lhs = jnp.concatenate([ah, al], 0 if ta else 1)
    if tb:
        rhs = jnp.concatenate(
            [jnp.concatenate([bh, bh], 1), jnp.concatenate([bl, bl], 1)], 0
        )
    else:
        row = jnp.concatenate([bh, bl], 1)
        rhs = jnp.concatenate([row, row], 0)
    out = lax.dot_general(
        lhs,
        rhs,
        (((0 if ta else 1,), (1 if tb else 0,)), ((), ())),
        preferred_element_type=F32,
    )
    n = out.shape[1] // 2
    return out[:, :n] + out[:, n:]


def ones_mm(ones, x):
    hi, mid = split(x)
    low = (x - hi.astype(F32) - mid.astype(F32)).astype(BF16)
    n = x.shape[1]
    out = jnp.dot(
        ones.astype(BF16), jnp.concatenate([hi, mid, low], 1), preferred_element_type=F32
    )
    return out[:, :n] + out[:, n : 2 * n] + out[:, 2 * n :]


def sigmoid(x):
    return 1.0 / (1.0 + jnp.exp(-x))


def softplus(x):
    return jnp.maximum(x, 0.0) + jnp.log1p(jnp.exp(-jnp.abs(x)))


def iotas(size):
    r = lax.broadcasted_iota(jnp.int32, (size, size), 0)
    c = lax.broadcasted_iota(jnp.int32, (size, size), 1)
    return r, c


def conv_pre(ext, x_ref, halo_ref, w_ref, j, cols):
    size = x_ref.shape[0]
    ext[0:PAD, :] = halo_ref[j, :, cols].astype(F32)
    ext[PAD : PAD + size, :] = x_ref[:, cols].astype(F32)
    taps = w_ref.shape[1]
    rows = [ext[PAD - taps + 1 + i : PAD - taps + 1 + i + size, :] for i in range(taps)]
    pre = w_ref[j, 0:1, cols] * rows[0]
    for i in range(1, taps):
        pre = pre + w_ref[j, i : i + 1, cols] * rows[i]
    return pre, rows


def pick_column(ref, index):
    row = ref[pl.ds(index, 1), :]
    r, c = iotas(row.shape[1])
    return jnp.sum(jnp.where(r == c, row, 0.0), axis=1, keepdims=True)


def unit(x):
    r = lax.rsqrt(jnp.sum(x * x, axis=1, keepdims=True) + EPS)
    return x * r, r


def decays(gate, dlog):
    size = gate.shape[0]
    half = size // 2
    r, c = iotas(size)
    speed = -jnp.exp(dlog)
    ld = speed * softplus(gate)
    cum = ones_mm(jnp.where(r >= c, 1.0, 0.0), ld)
    row = lax.broadcasted_iota(jnp.int32, gate.shape, 0)
    first = row < half
    mid = jnp.where(
        first, cum[half // 2 : half // 2 + 1, :], cum[half + half // 2 : half + half // 2 + 1, :]
    )
    edge = cum[half - 1 : half, :]
    last = cum[size - 1 : size, :]
    up = jnp.exp(cum - mid)
    down = jnp.exp(mid - cum)
    cross = jnp.exp(jnp.where(first, edge - cum, cum - edge))
    full = jnp.exp(cum)
    end = jnp.exp(last - cum)
    return ld, speed, up, down, cross, full, end, jnp.exp(last), first


def pair_scores(qk_up, k_down, qk_cross, k_cross):
    size = k_down.shape[0]
    half = size // 2
    same = mm(qk_up, k_down, tb=True)
    other = mm(qk_cross, k_cross, tb=True)
    r, c = iotas(size)
    same_half = (r < half) == (c < half)
    return (
        jnp.where(same_half, same[:size], other[:size]),
        jnp.where(same_half, same[size:], other[size:]),
    )


def unit_inverses(coups):
    size = coups[0].shape[0]
    r, c = iotas(size)
    ident = jnp.where(r == c, 1.0, 0.0)
    shift = 3
    inside = (r >> shift) == (c >> shift)
    small = [jnp.where(inside, a, 0.0) for a in coups]
    p2 = [mm(a, a) for a in small]
    base = [ident - a for a in small]
    p4 = [mm(p, p) for p in p2]
    base = [x + mm(x, p) for x, p in zip(base, p2)]
    d = [x + mm(x, p) for x, p in zip(base, p4)]
    while (1 << shift) < size:
        joined = ((r >> (shift + 1)) == (c >> (shift + 1))) & ((r >> shift) != (c >> shift))
        low = [mm(jnp.where(joined, a, 0.0), x) for a, x in zip(coups, d)]
        d = [x - mm(x, y) for x, y in zip(d, low)]
        shift += 1
    return d


def scan_kernel(
    group,
    q_ref, k_ref, v_ref, gate_ref, beta_ref, w_ref, dlog_ref, grad_ref,
    halo_ref, inv_ref, raw_ref, att_ref, reach_ref, state_ref, cotan_ref,
    ext, halo_in, trans, offset, adjoint,
    gt, gb, ga, pre_t, pre_b, send_s, send_g, in_s, in_g, out_s, out_g, back_s, back_g,
    hs, hr, at_s, at_r, ab_s, ab_r, aa_s, aa_r, ss, rs, sg, rg, bs_s, bs_r, bg_s, bg_r,
):
    n = lax.axis_size("seq")
    me = lax.axis_index("seq")
    team, mine_heads = gt.shape[0], gt.shape[1]
    mine = lax.rem(me, team)
    base = me - mine
    level = me // team
    levels = n // team
    mesh_id = pl.DeviceIdType.MESH
    right = lax.rem(me + 1, n)
    left = lax.rem(me + n - 1, n)
    after = lax.rem(me + team, n)
    ahead = lax.rem(me + n - team, n)
    barrier = pltpu.get_barrier_semaphore()
    peers = [base + lax.rem(mine + i, team) for i in range(1, team)]
    links = peers + [right, left] + ([after, ahead] if levels > 1 else [])
    for peer in links:
        pl.semaphore_signal(barrier, inc=1, device_id={"seq": peer}, device_id_type=mesh_id)
    pl.semaphore_wait(barrier, len(links))

    size = q_ref.shape[0]
    heads, width = trans.shape[0], trans.shape[1]

    def halo_copy(j, ref):
        return pltpu.make_async_remote_copy(
            src_ref=ref.at[pl.ds(size - PAD, PAD)], dst_ref=halo_in.at[j],
            send_sem=hs.at[j], recv_sem=hr.at[j],
            device_id={"seq": right}, device_id_type=mesh_id,
        )

    @pl.when(me < n - 1)
    def _():
        for j, ref in enumerate((q_ref, k_ref, v_ref)):
            halo_copy(j, ref).start()

    def block(member):
        return pl.ds(member * mine_heads, mine_heads)

    def spread(source, target, ref, dst, send, recv):
        return pltpu.make_async_remote_copy(
            src_ref=ref.at[block(target)], dst_ref=dst.at[source],
            send_sem=send.at[target], recv_sem=recv.at[source],
            device_id={"seq": base + target}, device_id_type=mesh_id,
        )

    kinds = (
        (trans, gt, at_s, at_r), (offset, gb, ab_s, ab_r), (adjoint, ga, aa_s, aa_r)
    )
    others = [lax.rem(mine + i, team) for i in range(1, team)]
    order = others + [mine]
    r, c = iotas(size)
    rr, cc = iotas(width)
    for begin in range(0, heads, group):
        held = []
        places = []
        for g in range(group):
            at = begin + g
            head = order[at // mine_heads] * mine_heads + at % mine_heads
            places.append((head, pl.ds(pl.multiple_of(head * width, width), width)))
        fades = [decays(gate_ref[:, cols], dlog_ref[:, cols]) for _, cols in places]
        if begin == 0:
            @pl.when(me == 0)
            def _():
                halo_in[...] = jnp.zeros_like(halo_in)

            @pl.when(me > 0)
            def _():
                for j, ref in enumerate((q_ref, k_ref, v_ref)):
                    halo_copy(j, ref).wait_recv()

            halo_ref[...] = halo_in[...]
        for g, (head, cols) in enumerate(places):
            pre_q, _ = conv_pre(ext.at[3 * g], q_ref, halo_in, w_ref, 0, cols)
            pre_k, _ = conv_pre(ext.at[3 * g + 1], k_ref, halo_in, w_ref, 1, cols)
            pre_v, _ = conv_pre(ext.at[3 * g + 2], v_ref, halo_in, w_ref, 2, cols)
            q, _ = unit(pre_q * sigmoid(pre_q))
            k, _ = unit(pre_k * sigmoid(pre_k))
            v = pre_v * sigmoid(pre_v)
            beta = sigmoid(pick_column(beta_ref, head))
            ld, speed, up, down, cross, full, end, dend, first = fades[g]
            kc = k * cross
            qk_up = jnp.concatenate([q * up, k * up], 0)
            qk_cross = jnp.concatenate([q * cross, kc], 0)
            att, raw = pair_scores(qk_up, k * down, qk_cross, kc)
            att = jnp.where(r >= c, att, 0.0)
            raw = jnp.where(r > c, raw, 0.0)
            raw_ref[head] = raw
            att_ref[head] = att
            reach_ref[head] = mm(att, grad_ref[:, cols].astype(F32), ta=True)
            inputs = jnp.concatenate([beta * k * full, beta * v], 1)
            held.append((raw * beta, inputs, k * end, dend, q * full))
        invs = unit_inverses([item[0] for item in held])
        bys = [mm(inv, item[1]) for inv, item in zip(invs, held)]
        for g, (head, cols) in enumerate(places):
            inv_ref[head] = invs[g]
            ends = mm(held[g][2], bys[g], ta=True)
            trans[head] = (jnp.where(rr == cc, held[g][3], 0.0) - ends[:, :width]).astype(LINK)
            offset[head] = ends[:, width:].astype(LINK)
            adjoint[head] = mm(
                jnp.concatenate([held[g][4], -bys[g][:, :width]], 0),
                jnp.concatenate([grad_ref[:, cols].astype(F32), reach_ref[head]], 0),
                ta=True,
            ).astype(LINK)
        for i in range(begin // mine_heads, (begin + group) // mine_heads):
            if i < len(others):
                for kind in kinds:
                    spread(mine, others[i], *kind).start()
    for ref, dst, _, _ in kinds:
        dst[mine] = ref[block(mine)]
    for kind in kinds[:2]:
        for other in others:
            spread(other, other, *kind).wait_recv()

    for h in range(mine_heads):
        pre_t[0, h] = gt[0, h].astype(F32)
        pre_b[0, h] = gb[0, h].astype(F32)
    for j in range(1, team):
        for h in range(mine_heads):
            both = mm(gt[j, h].astype(F32), jnp.concatenate([pre_t[j - 1, h], pre_b[j - 1, h]], 1))
            pre_t[j, h] = both[:, :width]
            pre_b[j, h] = both[:, width:] + gb[j, h].astype(F32)
    for other in others:
        spread(other, other, *kinds[2]).wait_recv()
    for h in range(mine_heads):
        send_g[h] = ga[team - 1, h].astype(F32)
    for j in range(team - 2, -1, -1):
        for h in range(mine_heads):
            send_g[h] = mm(gt[j, h].astype(F32), send_g[h], ta=True) + ga[j, h].astype(F32)

    def state_copy(h):
        return pltpu.make_async_remote_copy(
            src_ref=send_s.at[h], dst_ref=in_s.at[h], send_sem=ss.at[h], recv_sem=rs.at[h],
            device_id={"seq": after}, device_id_type=mesh_id,
        )

    def cotan_copy(h):
        return pltpu.make_async_remote_copy(
            src_ref=send_g.at[h], dst_ref=in_g.at[h], send_sem=sg.at[h], recv_sem=rg.at[h],
            device_id={"seq": ahead}, device_id_type=mesh_id,
        )

    def give(member, owner, src, dst, send, recv):
        return pltpu.make_async_remote_copy(
            src_ref=src.at[member], dst_ref=dst.at[block(owner)],
            send_sem=send.at[member], recv_sem=recv.at[owner],
            device_id={"seq": base + member}, device_id_type=mesh_id,
        )

    states = (out_s, back_s, bs_s, bs_r)
    cotans = (out_g, back_g, bg_s, bg_r)

    def forward():
        for h in range(mine_heads):
            @pl.when(level == 0)
            def _():
                in_s[h] = jnp.zeros_like(in_s[h])
                send_s[h] = pre_b[team - 1, h]

            @pl.when(level > 0)
            def _():
                state_copy(h).wait_recv()
                state = in_s[h]

                @pl.when(level < levels - 1)
                def _():
                    send_s[h] = mm(pre_t[team - 1, h], state) + pre_b[team - 1, h]

            @pl.when(level < levels - 1)
            def _():
                state_copy(h).start()

        for h in range(mine_heads):
            state = in_s[h]
            out_s[0, h] = state.astype(LINK)
            for j in range(1, team):
                out_s[j, h] = (mm(pre_t[j - 1, h], state) + pre_b[j - 1, h]).astype(LINK)
        for other in others:
            give(other, mine, *states).start()

    def backward():
        for h in range(mine_heads):
            @pl.when(level == levels - 1)
            def _():
                in_g[h] = jnp.zeros_like(in_g[h])

            @pl.when(level < levels - 1)
            def _():
                cotan_copy(h).wait_recv()
                cotan = in_g[h]

                @pl.when(level > 0)
                def _():
                    send_g[h] = mm(pre_t[team - 1, h], cotan, ta=True) + send_g[h]

            @pl.when(level > 0)
            def _():
                cotan_copy(h).start()

        cotans_at = [in_g[h] for h in range(mine_heads)]
        for j in range(team - 1, -1, -1):
            for h in range(mine_heads):
                out_g[j, h] = cotans_at[h].astype(LINK)
                if j:
                    cotans_at[h] = mm(gt[j, h].astype(F32), cotans_at[h], ta=True) + ga[
                        j, h
                    ].astype(F32)

        for other in others:
            give(other, mine, *cotans).start()

    @pl.when(level < levels // 2)
    def _():
        forward()
        backward()

    @pl.when(level >= levels // 2)
    def _():
        backward()
        forward()

    back_s[block(mine)] = out_s[mine]
    back_g[block(mine)] = out_g[mine]
    for other in others:
        give(mine, other, *states).wait_recv()
    for other in others:
        give(mine, other, *cotans).wait_recv()
    state_ref[...] = back_s[...].astype(F32)
    cotan_ref[...] = back_g[...].astype(F32)
    for other in others:
        for kind in kinds:
            spread(mine, other, *kind).wait_send()
        give(other, mine, *states).wait_send()
        give(other, mine, *cotans).wait_send()
    for h in range(mine_heads):
        @pl.when(level < levels - 1)
        def _():
            state_copy(h).wait_send()

        @pl.when(level > 0)
        def _():
            cotan_copy(h).wait_send()

    @pl.when(me < n - 1)
    def _():
        for j, ref in enumerate((q_ref, k_ref, v_ref)):
            halo_copy(j, ref).wait_send()


def grads_kernel(
    group,
    q_ref, k_ref, v_ref, halo_ref, gate_ref, beta_ref, w_ref, dlog_ref, grad_ref,
    inv_ref, raw_ref, att_ref, reach_ref, state_ref, cotan_ref,
    dq_ref, dk_ref, dv_ref, dgate_ref, dbeta_ref, red_ref, tail_ref, last_ref,
    ext, dext,
):
    size = q_ref.shape[0]
    half = size // 2
    width = state_ref.shape[1]
    taps = w_ref.shape[1]
    r, c = iotas(size)
    same_half = (r < half) == (c < half)
    for g in range(group):
        cols = slice(g * width, (g + 1) * width)
        head = pl.program_id(0) * group + g
        pres, rows = [], []
        for j, ref in enumerate((q_ref, k_ref, v_ref)):
            pre, row = conv_pre(ext.at[3 * g + j], ref, halo_ref, w_ref, j, cols)
            pres.append(pre)
            rows.append(row)
        sig = [sigmoid(pre) for pre in pres]
        q, q_r = unit(pres[0] * sig[0])
        k, k_r = unit(pres[1] * sig[1])
        v = pres[2] * sig[2]
        beta = sigmoid(pick_column(beta_ref, head))
        gate = gate_ref[:, cols]
        ld, speed, up, down, cross, full, end, dend, first = decays(gate, dlog_ref[:, cols])
        inv, raw, att, reach = inv_ref[g], raw_ref[g], att_ref[g], reach_ref[g]
        state, cotan = state_ref[g], cotan_ref[g]
        grad = grad_ref[:, cols].astype(F32)

        resid = v - mm(k * full, state)
        deltas = mm(inv, beta * resid)
        d_deltas = reach + mm(k * end, cotan)
        d_err = mm(inv, d_deltas, ta=True)
        d_v = beta * d_err
        stacked = jnp.concatenate([grad, -d_v], 0)
        to_full = mm(stacked, state, tb=True)
        d_qf, d_kf = to_full[:size], to_full[size:]
        scores = mm(jnp.concatenate([grad, -d_err], 0), deltas, tb=True)
        d_att = jnp.where(r >= c, scores[:size], 0.0)
        d_coup = jnp.where(r > c, scores[size:], 0.0)
        d_ke = mm(deltas, cotan, tb=True)
        d_beta = jnp.sum(d_err * resid, axis=1, keepdims=True) + jnp.sum(
            d_coup * raw, axis=1, keepdims=True
        )
        d_raw = d_coup * beta
        kc = k * cross
        both = jnp.concatenate([d_att, d_raw], 0)
        same2 = jnp.concatenate([same_half, same_half], 0)
        d_same = jnp.where(same2, both, 0.0)
        d_other = jnp.where(same2, 0.0, both)
        from_same = mm(d_same, k * down)
        from_other = mm(d_other, kc)
        to_down = mm(d_same, jnp.concatenate([q * up, k * up], 0), ta=True)
        to_cross = mm(d_other, jnp.concatenate([q * cross, kc], 0), ta=True)
        d_q = from_same[:size] * up + from_other[:size] * cross + d_qf * full
        d_k_up = from_same[size:] * up + from_other[size:] * cross + d_kf * full
        k_end_part = d_ke * end
        d_k_down = to_down * down + to_cross * cross + k_end_part
        d_k = d_k_up + d_k_down
        d_cum = q * d_q + k * (d_k_up - d_k_down)
        ones_row = jnp.ones((8, width), F32)
        end_state = mm(ones_row, state * cotan, tb=True)[0:1, :]
        d_last = jnp.sum(k * k_end_part, axis=0, keepdims=True) + dend * end_state
        d_ld = ones_mm(jnp.where(c >= r, 1.0, 0.0), d_cum) + d_last
        dgate_ref[:, cols] = speed * sigmoid(gate) * d_ld
        d_dlog = jnp.sum(ld * d_ld, axis=0, keepdims=True)
        d_braw = d_beta * beta * (1.0 - beta)
        dbeta_ref[pl.ds(head, 1), :] = jnp.sum(
            jnp.where(r == c, d_braw, 0.0), axis=0, keepdims=True
        )

        d_q = q_r * (d_q - q * jnp.sum(q * d_q, axis=1, keepdims=True))
        d_k = k_r * (d_k - k * jnp.sum(k * d_k, axis=1, keepdims=True))
        red = []
        for j, (d_act, out_ref) in enumerate(((d_q, dq_ref), (d_k, dk_ref), (d_v, dv_ref))):
            s = sig[j]
            d_pre = d_act * (s * (1.0 + pres[j] * (1.0 - s)))
            spot = dext.at[3 * g + j]
            spot[0:PAD, :] = jnp.zeros((PAD, width), F32)
            spot[PAD : PAD + size, :] = d_pre
            spot[PAD + size :, :] = jnp.zeros((PAD, width), F32)
            whole = None
            tail = None
            for i in range(taps):
                w = w_ref[j, i : i + 1, cols]
                start = PAD + taps - 1 - i
                term = w * spot[start : start + size, :]
                edge = w * spot[taps - 1 - i : taps - 1 - i + PAD, :]
                whole = term if whole is None else whole + term
                tail = edge if tail is None else tail + edge
                red.append(jnp.sum(d_pre * rows[j][i], axis=0, keepdims=True))
            out_ref[:, cols] = whole.astype(BF16)
            tail_ref[j, :, cols] = tail
            last_ref[j, :, cols] = whole[size - PAD :, :]
        red.append(d_dlog)
        red.append(jnp.zeros((RED - len(red), width), F32))
        red_ref[g * RED : (g + 1) * RED, :] = jnp.concatenate(red, 0)


def finish_kernel(
    red_ref, tail_ref, conv_ref, decay_ref, after_ref,
    parts, mine, result, tail_in, s1, r1, s2, r2, st, rt,
):
    n = lax.axis_size("seq")
    me = lax.axis_index("seq")
    owners = min(n, red_ref.shape[0] // 8)
    piece = red_ref.shape[0] // owners
    right = lax.rem(me + 1, n)
    left = lax.rem(me + n - 1, n)
    mesh_id = pl.DeviceIdType.MESH
    barrier = pltpu.get_barrier_semaphore()

    @pl.loop(1, n)
    def _(step):
        pl.semaphore_signal(
            barrier, inc=1, device_id={"seq": lax.rem(me + step, n)}, device_id_type=mesh_id
        )

    pl.semaphore_wait(barrier, n - 1)

    def rows(owner):
        return pl.ds(pl.multiple_of(owner * piece, 8), piece)

    tail_copy = pltpu.make_async_remote_copy(
        src_ref=tail_ref, dst_ref=tail_in, send_sem=st, recv_sem=rt,
        device_id={"seq": left}, device_id_type=mesh_id,
    )

    def scatter(owner, source):
        return pltpu.make_async_remote_copy(
            src_ref=red_ref.at[rows(owner)], dst_ref=parts.at[source],
            send_sem=s1.at[owner], recv_sem=r1.at[source],
            device_id={"seq": owner}, device_id_type=mesh_id,
        )

    def spread(target, owner):
        return pltpu.make_async_remote_copy(
            src_ref=mine, dst_ref=result.at[rows(owner)],
            send_sem=s2.at[target], recv_sem=r2.at[owner],
            device_id={"seq": target}, device_id_type=mesh_id,
        )

    @pl.loop(0, owners)
    def _(owner):
        @pl.when(owner != me)
        def _():
            scatter(owner, me).start()

    tail_copy.start()

    @pl.when(me < owners)
    def _():
        mine[...] = red_ref[rows(lax.rem(me, owners)), :]

        @pl.loop(0, n)
        def _(source):
            @pl.when(source != me)
            def _():
                scatter(lax.rem(me, owners), source).wait_recv()
                mine[...] += parts[source]

        @pl.loop(1, n)
        def _(step):
            spread(lax.rem(me + step, n), lax.rem(me, owners)).start()

        result[rows(lax.rem(me, owners)), :] = mine[...]

    @pl.loop(0, owners)
    def _(owner):
        @pl.when(owner != me)
        def _():
            spread(me, owner).wait_recv()

    width = result.shape[1]
    taps = conv_ref.shape[1]
    for h in range(result.shape[0] // RED):
        cols = slice(h * width, (h + 1) * width)
        for j in range(3):
            start = h * RED + j * taps
            conv_ref[j, :, cols] = result[start : start + taps, :]
        start = h * RED + 3 * taps
        decay_ref[:, cols] = result[start : start + 1, :]
    tail_copy.wait_recv()
    after_ref[...] = jnp.where(me == n - 1, 0.0, tail_in[...])

    @pl.loop(0, owners)
    def _(owner):
        @pl.when(owner != me)
        def _():
            scatter(owner, me).wait_send()

    @pl.when(me < owners)
    def _():
        @pl.loop(1, n)
        def _(step):
            spread(lax.rem(me + step, n), lax.rem(me, owners)).wait_send()

    tail_copy.wait_send()


def per_device(query_raw, key_raw, value_raw, gate_raw, beta_raw, conv_weight, decay_log, grad_out):
    n = lax.axis_size("seq")
    size, channels = gate_raw.shape
    heads = beta_raw.shape[1]
    width = channels // heads
    group = GROUP if heads % GROUP == 0 else 1
    steps = heads // group
    span = group * width
    dlog = decay_log.reshape(1, channels)
    vmem = pl.BlockSpec(memory_space=pltpu.VMEM)
    tokens = pl.BlockSpec((size, span), lambda h: (0, h))
    rows8 = pl.BlockSpec((3, PAD, span), lambda h: (0, 0, h))
    betas = pl.BlockSpec((heads, size), lambda h: (0, 0))
    weights = pl.BlockSpec((3, conv_weight.shape[1], span), lambda h: (0, 0, h))
    single = pl.BlockSpec((1, span), lambda h: (0, h))
    square = pl.BlockSpec((group, width, width), lambda h: (h, 0, 0))
    pairs = pl.BlockSpec((group, size, size), lambda h: (h, 0, 0))
    tall = pl.BlockSpec((group, size, width), lambda h: (h, 0, 0))
    sq = jax.ShapeDtypeStruct((heads, width, width), F32)
    pr = jax.ShapeDtypeStruct((heads, size, size), F32)
    tl = jax.ShapeDtypeStruct((heads, size, width), F32)
    params = pltpu.CompilerParams(vmem_limit_bytes=VMEM_LIMIT)
    team = math.gcd(TEAM, math.gcd(n, heads))
    part = heads // team
    block = GROUP_MAPS if heads % GROUP_MAPS == 0 and GROUP_MAPS % part == 0 else heads
    whole = pltpu.VMEM((heads, width, width), LINK)
    few = pltpu.VMEM((part, width, width), F32)
    many = pltpu.VMEM((team, part, width, width), LINK)
    wide = pltpu.VMEM((team, part, width, width), F32)
    sems = pltpu.SemaphoreType.DMA((team,))
    hops = pltpu.SemaphoreType.DMA((part,))
    three = pltpu.SemaphoreType.DMA((3,))
    head_args = (query_raw, key_raw, value_raw)
    tail_args = (gate_raw, beta_raw.T, conv_weight, dlog, grad_out)
    halo, inv, raw, att, reach, state, cotan = pl.pallas_call(
        functools.partial(scan_kernel, block),
        out_shape=(
            jax.ShapeDtypeStruct((3, PAD, channels), query_raw.dtype), pr, pr, pr, tl, sq, sq,
        ),
        in_specs=[vmem] * 8,
        out_specs=(vmem,) * 7,
        scratch_shapes=[
            pltpu.VMEM((3 * block, PAD + size, width), F32),
            pltpu.VMEM((3, PAD, channels), query_raw.dtype),
        ]
        + [whole] * 3 + [many] * 3 + [wide] * 2 + [few] * 4 + [many] * 2 + [whole] * 2
        + [three] * 2 + [sems] * 6 + [hops] * 4 + [sems] * 4,
        compiler_params=pltpu.CompilerParams(
            collective_id=0, has_side_effects=True, vmem_limit_bytes=VMEM_LIMIT
        ),
        name="scan",
    )(*head_args, *tail_args)
    common = head_args + (halo,) + tail_args
    common_specs = [
        tokens, tokens, tokens, rows8, tokens, betas, weights, single, tokens,
    ]

    act = jax.ShapeDtypeStruct((size, channels), BF16)
    edge = jax.ShapeDtypeStruct((3, PAD, channels), F32)
    dq, dk, dv, dgate, dbeta, red, tail, last = pl.pallas_call(
        functools.partial(grads_kernel, group),
        grid=(steps,),
        out_shape=(
            act, act, act,
            jax.ShapeDtypeStruct((size, channels), F32),
            jax.ShapeDtypeStruct((heads, size), F32),
            jax.ShapeDtypeStruct((heads * RED, width), F32),
            edge, edge,
        ),
        in_specs=common_specs + [pairs, pairs, pairs, tall, square, square],
        out_specs=(
            tokens, tokens, tokens, tokens, betas,
            pl.BlockSpec((group * RED, width), lambda h: (h, 0)),
            rows8, rows8,
        ),
        scratch_shapes=[
            pltpu.VMEM((3 * group, PAD + size, width), F32),
            pltpu.VMEM((3 * group, PAD + size + PAD, width), F32),
        ],
        compiler_params=params,
        name="grads",
    )(*common, inv, raw, att, reach, state, cotan)

    owners = min(n, heads * RED // 8)
    piece = heads * RED // owners
    conv_sum, decay_sum, after = pl.pallas_call(
        finish_kernel,
        out_shape=(
            jax.ShapeDtypeStruct(conv_weight.shape, F32),
            jax.ShapeDtypeStruct((1, channels), F32),
            edge,
        ),
        in_specs=[vmem] * 2,
        out_specs=(vmem, vmem, vmem),
        scratch_shapes=[
            pltpu.VMEM((n, piece, width), F32),
            pltpu.VMEM((piece, width), F32),
            pltpu.VMEM(red.shape, F32),
            pltpu.VMEM(edge.shape, F32),
            pltpu.SemaphoreType.DMA((owners,)),
            pltpu.SemaphoreType.DMA((n,)),
            pltpu.SemaphoreType.DMA((n,)),
            pltpu.SemaphoreType.DMA((owners,)),
            pltpu.SemaphoreType.DMA,
            pltpu.SemaphoreType.DMA,
        ],
        compiler_params=pltpu.CompilerParams(
            collective_id=1, has_side_effects=True, vmem_limit_bytes=VMEM_LIMIT
        ),
        name="finish",
    )(red, tail)

    ends = (last + after).astype(BF16)
    dq = lax.dynamic_update_slice(dq, ends[0], (size - PAD, 0))
    dk = lax.dynamic_update_slice(dk, ends[1], (size - PAD, 0))
    dv = lax.dynamic_update_slice(dv, ends[2], (size - PAD, 0))
    return (dq, dk, dv, dgate, dbeta.T, conv_sum, decay_sum.reshape(channels))


def solution(mesh):
    in_specs = (
        P("seq", "head"),
        P("seq", "head"),
        P("seq", "head"),
        P("seq", "head"),
        P("seq", "head"),
        P(None, None, "head"),
        P("head"),
        P("seq", "head"),
    )
    out_specs = (
        P("seq", "head"),
        P("seq", "head"),
        P("seq", "head"),
        P("seq", "head"),
        P("seq", "head"),
        P(None, None, "head"),
        P("head"),
    )
    return jax.shard_map(
        per_device, mesh=mesh, in_specs=in_specs, out_specs=out_specs, check_vma=False
    )
```

profile of v0, /device:TPU:0, one launch (start us, length us, event | category | flops | bytes accessed | tf_op | source)
XLA Modules:
  0.0 83.8 jit_solution(7329922464065297071)
XLA Ops:
  0.6 52.5 %scan.1 = (bf16[3,8,1024]{2,1,0:T(8,128)(2,1)}, f32[8,128,128]{2,1,0:T(8,128)}, f32[8,128,128]{2,1,0:T(8,128)}, f32[8,128,128]{2,1,0:T(8,128)}, f32[8,128,128]{2...) custom-call(bf16[128,1024]{1,0:T(8,128)(2,1)} %q_ref.3, bf16[128,1024]{1,0:T(8,128)(2,1)} %k_ref.3, ...), custom_call_target="tpu_custom_call" | custom-call | tf_op jit(solution)/shard_map/scan/pallas_call | solution.py:643
  53.1 12.7 %grads.1 = (bf16[128,1024]{1,0:T(8,128)(2,1)}, bf16[128,1024]{1,0:T(8,128)(2,1)}, bf16[128,1024]{1,0:T(8,128)(2,1)}, f32[128,1024]{1,0:T(8,128)}, f32[8,128]{1,0...) custom-call(bf16[128,1024]{1,0:T(8,128)(2,1)} %q_ref.3, bf16[128,1024]{1,0:T(8,128)(2,1)} %k_ref.3, ...), custom_call_target="tpu_custom_call" | custom-call | tf_op jit(solution)/shard_map/grads/pallas_call | solution.py:668
  65.8 0.0 copy-start
  65.8 15.0 %finish.1 = (f32[3,4,1024]{2,1,0:T(4,128)}, f32[1,1024]{1,0:T(1,128)}, f32[3,8,1024]{2,1,0:T(8,128)}) custom-call(f32[128,128]{1,0:T(8,128)} %get-tuple-element.34.red_ref, f32[3,8,1024]{2,1,0:T(8,128)} %get-tuple-element.35.tail_ref), custom_call_target="tpu_custom_call" | custom-call | tf_op jit(solution)/shard_map/finish/pallas_call | solution.py:694
  80.8 0.0 copy-done
  80.8 0.9 %add_convert_fusion = bf16[3,8,1024]{2,1,0:T(8,128)(2,1)S(1)} fusion(f32[3,8,1024]{2,1,0:T(8,128)S(1)} %copy-done, f32[3,8,1024]{2,1,0:T(8,128)} %get-tuple-element.36), kind=kLoop, calls=%fused_computation | loop fusion | flops 49152 | bytes 245760 | tf_op jit(solution)/shard_map/convert_element_type | solution.py:721
  81.7 0.0 copy-start.1
  81.7 0.6 fusion
  82.3 0.2 copy-done.1
  82.5 0.0 copy-start.2
  82.5 0.6 copy.20
  83.1 0.1 copy-done.2
  83.2 0.6 copy.21
Async XLA Ops:
  65.8 15.0 %copy-start = (f32[3,8,1024]{2,1,0:T(8,128)S(1)}, f32[3,8,1024]{2,1,0:T(8,128)}, u32[]{:S(2)}) copy-start(f32[3,8,1024]{2,1,0:T(8,128)} %get-tuple-element.33) | copy-start | bytes 294916
  81.7 0.8 copy-start.1
  82.5 0.7 copy-start.2
where the time goes:
time: 84.1 us; the launch traced here: 83.8 us
  Pallas kernels  80.1 us (95%)
  local copies, waits for them, and re-layouts  2.06 us (2%)
  other arithmetic  0.91 us (1%)
    pallas_call x1, Pallas kernels, per_device(): pl.pallas_call(functools.partial(scan_kernel, block), out_shape=(jax.Shap...  52.5 us
    pallas_call x1, Pallas kernels, per_device(): pl.pallas_call(finish_kernel, out_shape=(jax.ShapeDtypeStruct(conv_weight...  15 us
    pallas_call x1, Pallas kernels, per_device(): pl.pallas_call(functools.partial(grads_kernel, group), grid=(steps,), out...  12.7 us

commit v1 on v0

v1 whole, which is shorter than its diff:
```python
import functools
import math

import jax
import jax.numpy as jnp
from jax import lax
from jax.experimental import pallas as pl
from jax.experimental.pallas import tpu as pltpu
from jax.sharding import PartitionSpec as P

F32 = jnp.float32
BF16 = jnp.bfloat16
EPS = 1e-06
PAD = 8
RED = 16
LAST = 16
GROUP = 2
TEAM = 8
VMEM_LIMIT = 64000000


def split(x):
    hi = x.astype(BF16)
    return hi, (x - hi.astype(F32)).astype(BF16)


def pack(x):
    return jnp.concatenate(split(x), 1)


def fold(out):
    n = out.shape[1] // 2
    return out[:, :n] + out[:, n:]


def dot(a, b, ta=False, tb=False):
    return lax.dot_general(
        a, b, (((0 if ta else 1,), (1 if tb else 0,)), ((), ())), preferred_element_type=F32
    )


def twice(x):
    return jnp.concatenate([x, x], 0)


def tall(x):
    n = x.shape[1] // 2
    return jnp.concatenate([x[:, :n], x[:, n:]], 0)


def cross_rows(x):
    n = x.shape[1] // 2
    hi, lo = x[:, :n], x[:, n:]
    return jnp.concatenate(
        [jnp.concatenate([hi, hi], 1), jnp.concatenate([lo, lo], 1)], 0
    )


def nn(a, b):
    return fold(dot(a, twice(b)))


def nt(a, b):
    return fold(dot(a, cross_rows(b), tb=True))


def tn(a, b):
    return fold(dot(tall(a), twice(b), ta=True))


def mm(a, b):
    return nn(pack(a), pack(b))


def ones_mm(ones, x, parts):
    rest, terms = x, []
    for _ in range(parts):
        term = rest.astype(BF16)
        terms.append(term)
        rest = rest - term.astype(F32)
    n = x.shape[1]
    out = jnp.dot(ones.astype(BF16), jnp.concatenate(terms, 1), preferred_element_type=F32)
    total = out[:, :n]
    for i in range(1, parts):
        total = total + out[:, i * n : (i + 1) * n]
    return total


def sigmoid(x):
    return 1.0 / (1.0 + jnp.exp(-x))


def softplus(x):
    return jnp.maximum(x, 0.0) + jnp.log1p(jnp.exp(-jnp.abs(x)))


def iotas(size):
    r = lax.broadcasted_iota(jnp.int32, (size, size), 0)
    c = lax.broadcasted_iota(jnp.int32, (size, size), 1)
    return r, c


def conv_pre(ext, x_ref, halo_ref, w_ref, j, cols):
    size = x_ref.shape[0]
    ext[0:PAD, :] = halo_ref[j, :, cols].astype(F32)
    ext[PAD : PAD + size, :] = x_ref[:, cols].astype(F32)
    taps = w_ref.shape[1]
    pre = None
    for i in range(taps):
        start = PAD - taps + 1 + i
        term = w_ref[j, i : i + 1, cols] * ext[start : start + size, :]
        pre = term if pre is None else pre + term
    return pre


def pick_column(ref, index):
    row = ref[pl.ds(index, 1), :]
    r, c = iotas(row.shape[1])
    return jnp.sum(jnp.where(r == c, row, 0.0), axis=1, keepdims=True)


def unit(x):
    r = lax.rsqrt(jnp.sum(x * x, axis=1, keepdims=True) + EPS)
    return x * r, r


def decays(gate, dlog):
    size = gate.shape[0]
    half = size // 2
    r, c = iotas(size)
    speed = -jnp.exp(dlog)
    ld = speed * softplus(gate)
    cum = ones_mm(jnp.where(r >= c, 1.0, 0.0), ld, 3)
    row = lax.broadcasted_iota(jnp.int32, gate.shape, 0)
    first = row < half
    mid = jnp.where(
        first, cum[half // 2 : half // 2 + 1, :], cum[half + half // 2 : half + half // 2 + 1, :]
    )
    edge = cum[half - 1 : half, :]
    last = cum[size - 1 : size, :]
    up = jnp.exp(cum - mid)
    down = jnp.exp(mid - cum)
    cross = jnp.exp(jnp.where(first, edge - cum, cum - edge))
    full = jnp.exp(cum)
    end = jnp.exp(last - cum)
    return ld, speed * sigmoid(gate), up, down, cross, full, end, jnp.exp(last)


def unit_inverses(coups):
    size = coups[0].shape[0]
    r, c = iotas(size)
    ident = jnp.where(r == c, 1.0, 0.0)
    shift = 3
    inside = (r >> shift) == (c >> shift)
    small = [jnp.where(inside, a, 0.0) for a in coups]
    p2 = [mm(a, a) for a in small]
    base = [ident - a for a in small]
    p4 = [mm(p, p) for p in p2]
    base = [x + mm(x, p) for x, p in zip(base, p2)]
    d = [x + mm(x, p) for x, p in zip(base, p4)]
    while (1 << shift) < size:
        joined = ((r >> (shift + 1)) == (c >> (shift + 1))) & ((r >> shift) != (c >> shift))
        low = [mm(jnp.where(joined, a, 0.0), x) for a, x in zip(coups, d)]
        d = [x - mm(x, y) for x, y in zip(d, low)]
        shift += 1
    return d


NAMES = (
    "q", "k", "v", "up", "down", "cross", "full", "end", "ld", "slope", "beta",
    "sq", "sk", "sv", "qr", "kr", "raw", "u", "reach",
)


def meet(start, step, count):
    if count & (count - 1):
        return lax.rem(start + step, count)
    out, bit = 0, 1
    while bit < count:
        out = out + lax.rem(start // bit + step // bit, 2) * bit
        bit *= 2
    return out


def layer_kernel(
    group,
    q_hbm, k_hbm, v_hbm, gate_hbm, beta_hbm, w_hbm, dlog_hbm, grad_hbm,
    dq_ref, dk_ref, dv_ref, dgate_ref, dbeta_ref, conv_ref, decay_ref,
    q_ref, k_ref, v_ref, gate_ref, beta_ref, w_ref, dlog_ref, grad_ref, load,
    keep, wk, ki, kd, kc, ups, crs, inv_sp, ke_sp, dend_row,
    ext, dext, halo_in,
    map_out, off_out, map_in, off_in, out_s, out_g, state_in, cotan_in,
    in_s, in_g, send_s, send_g,
    red_level, red_team, tail_out, tail_in, last_rows,
    hs, hr, ms, mr, fs, fr, ss, sr, gs, gr, cs, cr, ds, dr, ts, tr, ls, lr, es, er,
):
    n = lax.axis_size("seq")
    me = lax.axis_index("seq")
    team, part = map_in.shape[0], map_in.shape[1]
    mine = lax.rem(me, team)
    base = me - mine
    level = me // team
    levels = n // team
    mesh_id = pl.DeviceIdType.MESH
    right = lax.rem(me + 1, n)
    left = lax.rem(me + n - 1, n)
    size = q_ref.shape[0]
    half = size // 2
    heads, width = map_out.shape[0], map_out.shape[2]
    blocks = heads // group
    own_block = (mine * part) // group

    loads = [
        pltpu.make_async_copy(src, dst, load.at[i])
        for i, (src, dst) in enumerate((
            (q_hbm, q_ref), (k_hbm, k_ref), (v_hbm, v_ref), (gate_hbm, gate_ref),
            (dlog_hbm, dlog_ref), (w_hbm, w_ref), (beta_hbm, beta_ref), (grad_hbm, grad_ref),
        ))
    ]
    for copy in loads:
        copy.start()
    barrier = pltpu.get_barrier_semaphore()
    links = [base + lax.rem(mine + i, team) for i in range(1, team)]
    links += [lax.rem(me + i * team, n) for i in range(1, levels)]
    links += [right, left]
    for peer in links:
        pl.semaphore_signal(barrier, inc=1, device_id={"seq": peer}, device_id_type=mesh_id)
    for copy in loads:
        copy.wait()
    pl.semaphore_wait(barrier, len(links))

    def remote(src, dst, send, recv, to):
        return pltpu.make_async_remote_copy(
            src_ref=src, dst_ref=dst, send_sem=send, recv_sem=recv,
            device_id={"seq": to}, device_id_type=mesh_id,
        )

    def halo_copy(j, ref):
        return remote(
            ref.at[pl.ds(size - PAD, PAD)], halo_in.at[j], hs.at[j], hr.at[j], right
        )

    raws = (q_ref, k_ref, v_ref)

    @pl.when(me < n - 1)
    def _():
        for j, ref in enumerate(raws):
            halo_copy(j, ref).start()

    def block(member):
        return pl.ds(member * part, part)

    def lanes(head):
        return pl.ds(pl.multiple_of(head * width, width), width)

    def map_copy(source, target):
        return remote(
            map_out.at[block(target)], map_in.at[source], ms.at[target], mr.at[source],
            base + target,
        )

    def off_copy(source, target):
        return remote(
            off_out.at[block(target)], off_in.at[source], fs.at[target], fr.at[source],
            base + target,
        )

    def state_give(owner, member):
        return remote(
            out_s.at[member], state_in.at[block(owner)], ss.at[member], sr.at[owner],
            base + member,
        )

    def cotan_give(owner, member):
        return remote(
            out_g.at[member], cotan_in.at[block(owner)], gs.at[member], gr.at[owner],
            base + member,
        )

    state_hop = remote(send_s, in_s, cs, cr, lax.rem(me + team, n))
    cotan_hop = remote(send_g, in_g, ds, dr, lax.rem(me + n - team, n))

    def saved(head):
        spot = keep.at[head]
        return {name: spot.at[i] for i, name in enumerate(NAMES)}

    r, c = iotas(size)
    rr, cc = iotas(width)
    low = c < half

    @pl.when(me == 0)
    def _():
        halo_in[...] = jnp.zeros_like(halo_in)

    @pl.when(me > 0)
    def _():
        for j, ref in enumerate(raws):
            halo_copy(j, ref).wait_recv()

    def maps(step):
        start = meet(own_block, blocks - 1 - step, blocks) * group
        held = []
        for g in range(group):
            head = start + g
            cols = lanes(head)
            s = saved(head)
            ld, slope, up, down, cross, full, end, dend = decays(
                gate_ref[:, cols], dlog_ref[:, cols]
            )
            acts = []
            for j, ref in enumerate(raws):
                pre = conv_pre(ext.at[head * 3 + j], ref, halo_in, w_ref, j, cols)
                sig = sigmoid(pre)
                s[("sq", "sk", "sv")[j]][...] = sig * (1.0 + pre * (1.0 - sig))
                acts.append(pre * sig)
            q, qr = unit(acts[0])
            k, kr = unit(acts[1])
            v = acts[2]
            beta = jnp.broadcast_to(sigmoid(pick_column(beta_ref, head)), (size, width))
            for name, value in (
                ("q", q), ("k", k), ("v", v), ("up", up), ("down", down), ("cross", cross),
                ("full", full), ("end", end), ("ld", ld), ("slope", slope), ("beta", beta),
                ("qr", jnp.broadcast_to(qr, (size, width))),
                ("kr", jnp.broadcast_to(kr, (size, width))),
            ):
                s[name][...] = value
            dend_row[head] = jnp.broadcast_to(dend, (8, width))
            kfull = k * full
            ups_sp = pack(jnp.concatenate([q * up, k * up], 0))
            ups[head] = ups_sp
            kd_sp = pack(k * down)
            kd[head] = kd_sp
            kcross = k * cross
            kc_sp = pack(kcross)
            kc[head] = kc_sp
            crs_sp = pack(jnp.concatenate([(q * cross)[half:], kcross[half:]], 0))
            crs[head] = crs_sp
            same = nt(ups_sp, kd_sp)
            other = nt(crs_sp, kc_sp)
            rest = size - half
            att = jnp.concatenate(
                [same[:half], jnp.where(low[half:], other[:rest], same[half:size])], 0
            )
            raw = jnp.concatenate(
                [same[size : size + half], jnp.where(low[half:], other[rest:], same[size + half :])],
                0,
            )
            att = jnp.where(r >= c, att, 0.0)
            raw = jnp.where(r > c, raw, 0.0)
            s["raw"][...] = raw
            grad = grad_ref[:, cols]
            ah, al = split(att)
            both = dot(jnp.concatenate([ah, al], 1), grad, ta=True)
            reach = both[:size] + both[size:]
            s["reach"][...] = reach
            wk[head, size:, :] = pack(kfull)
            ke_sp[head] = pack(k * end)
            held.append((raw * beta, beta * kfull, beta * v, pack(q * full), reach, dend))
        invs = unit_inverses([item[0] for item in held])
        for g in range(group):
            head = start + g
            cols = lanes(head)
            s = saved(head)
            isp = pack(invs[g])
            inv_sp[head] = isp
            by = nn(isp, pack2(held[g][1], held[g][2]))
            s["u"][...] = by[:, width:]
            bh, bl = split(by)
            wsp = jnp.concatenate([bh[:, :width], bl[:, :width]], 1)
            wk[head, :size, :] = wsp
            ends = tn(ke_sp[head], jnp.concatenate([bh, bl], 1))
            full_map = jnp.where(rr == cc, held[g][5], 0.0) - ends[:, :width]
            map_hi = full_map.astype(BF16)
            left_over = jnp.sum(
                jnp.where(rr == cc, full_map - map_hi.astype(F32), 0.0), axis=0, keepdims=True
            )
            map_out[head, :width, :] = map_hi
            map_out[head, width:, :] = jnp.broadcast_to(left_over, (16, width)).astype(BF16)
            off_out[head, :width, :] = ends[:, width:]
            grad = grad_ref[:, cols]
            gsp = jnp.concatenate([grad, jnp.zeros_like(grad)], 1)
            off_out[head, width:, :] = tn(
                jnp.concatenate([held[g][3], -wsp], 0),
                jnp.concatenate([gsp, pack(held[g][4])], 0),
            )
        for g in range(group):
            head = start + g
            target = head // part

            @pl.when((target != mine) & (lax.rem(head, part) == part - 1))
            def _():
                map_copy(mine, target).start()
                off_copy(mine, target).start()

    for step in range(blocks):
        maps(step)
    map_in[mine] = map_out[block(mine)]
    off_in[mine] = off_out[block(mine)]

    def step_maps(j, h):
        both = map_in[j, h]
        rest = jnp.where(rr == cc, both[width : width + 1, :].astype(F32), 0.0).astype(BF16)
        return both[:width], rest

    def forward_step(j, h, state):
        hi, rest = step_maps(j, h)
        return nn(jnp.concatenate([hi, rest], 1), pack(state)) + off_in[j, h, :width, :]

    def backward_step(j, h, cotan):
        hi, rest = step_maps(j, h)
        out = fold(dot(jnp.concatenate([hi, rest], 0), twice(pack(cotan)), ta=True))
        return out + off_in[j, h, width:, :]

    def arrive(j):
        @pl.when(j != mine)
        def _():
            map_copy(j, j).wait_recv()
            off_copy(j, j).wait_recv()

    def forward(first):
        @pl.when(level == 0)
        def _():
            in_s[...] = jnp.zeros_like(in_s)

        @pl.when(level > 0)
        def _():
            state_hop.wait_recv()

        states = [in_s[h] for h in range(part)]
        for j in range(team):
            if first:
                arrive(j)
            for h in range(part):
                out_s[j, h] = states[h]
                states[h] = forward_step(j, h, states[h])

        @pl.when(level < levels - 1)
        def _():
            for h in range(part):
                send_s[h] = states[h]
            state_hop.start()

        state_in[block(mine)] = out_s[mine]
        for i in range(1, team):
            state_give(mine, meet(mine, i, team)).start()

    def backward(first):
        @pl.when(level == levels - 1)
        def _():
            in_g[...] = jnp.zeros_like(in_g)

        @pl.when(level < levels - 1)
        def _():
            cotan_hop.wait_recv()

        cotans = [in_g[h] for h in range(part)]
        for j in range(team - 1, -1, -1):
            if first:
                arrive(j)
            for h in range(part):
                out_g[j, h] = cotans[h]
                cotans[h] = backward_step(j, h, cotans[h])

        @pl.when(level > 0)
        def _():
            for h in range(part):
                send_g[h] = cotans[h]
            cotan_hop.start()

        cotan_in[block(mine)] = out_g[mine]
        for i in range(1, team):
            cotan_give(mine, meet(mine, i, team)).start()

    def ready(head):
        s = saved(head)
        isp = inv_sp[head]
        rh, rl = split(s["reach"][...])
        esp = ke_sp[head]
        rhs = jnp.concatenate([rh, esp[:, :width], rl, esp[:, width:]], 1)
        out = tn(isp, rhs)
        s["reach"][...] = out[:, :width]
        ki[head] = pack(out[:, width:])

    for head in range(heads // 2):
        ready(head)

    @pl.when(level < levels // 2)
    def _():
        forward(True)

    @pl.when(level >= levels // 2)
    def _():
        backward(True)

    for head in range(heads // 2, heads):
        ready(head)

    @pl.when(level < levels // 2)
    def _():
        backward(False)

    @pl.when(level >= levels // 2)
    def _():
        forward(False)

    def level_copy(b, source, target):
        spot = red_level.at[source, pl.ds(b * group, group)]
        return remote(
            spot, spot, ts.at[target, b], tr.at[source, b], lax.rem(target * team + mine, n)
        )

    def team_copy(b, source, target):
        spot = red_team.at[source, pl.ds(b * group, group)]
        return remote(spot, spot, ls.at[target, b], lr.at[source, b], base + target)

    def tail_copy(b):
        spot = pl.ds(b * group, group)
        return remote(tail_out.at[spot], tail_in.at[spot], es.at[b], er.at[b], left)

    other_levels = [lax.rem(level + i, levels) for i in range(1, levels)]
    others = [meet(mine, i, team) for i in range(1, team)]
    upper = jnp.where(c >= r, 1.0, 0.0)
    ones8 = jnp.ones((8, width), BF16)
    taps = w_ref.shape[1]

    def grads(b):
        for g in range(group):
            head = b * group + g
            owner = head // part

            @pl.when((owner != mine) & (lax.rem(head, part) == 0))
            def _():
                state_give(owner, owner).wait_recv()
                cotan_give(owner, owner).wait_recv()

        for g in range(group):
            head = b * group + g
            cols = lanes(head)
            s = saved(head)
            state, cotan = state_in[head], cotan_in[head]
            ssp, csp = pack(state), pack(cotan)
            wkx = nn(wk[head], ssp)
            deltas = s["u"][...] - wkx[:size]
            resid = s["v"][...] - wkx[size:]
            d_err = s["reach"][...] + nn(ki[head], csp)
            beta = s["beta"][...]
            d_v = beta * d_err
            grad = grad_ref[:, cols]
            esp = pack(d_err)
            lhs = jnp.concatenate(
                [jnp.concatenate([grad, jnp.zeros_like(grad)], 1), esp], 0
            )
            dsp = pack(deltas)
            to_full = nt(lhs, ssp)
            scores = nt(lhs, dsp)
            d_ke = nt(dsp, csp)
            d_att = jnp.where(r >= c, scores[:size], 0.0)
            d_coup = jnp.where(r > c, -scores[size:], 0.0)
            d_beta = jnp.sum(
                d_err * resid + d_coup * s["raw"][...], axis=1, keepdims=True
            )
            d_raw = d_coup * beta
            crossed = jnp.concatenate(
                [jnp.where(low[half:], d_att[half:], 0.0), jnp.where(low[half:], d_raw[half:], 0.0)],
                0,
            )
            both = jnp.concatenate(
                [
                    d_att[:half], jnp.where(low[half:], 0.0, d_att[half:]),
                    d_raw[:half], jnp.where(low[half:], 0.0, d_raw[half:]),
                ],
                0,
            )
            bsp, xsp = pack(both), pack(crossed)
            from_same = nn(bsp, kd[head])
            from_other = nn(xsp, kc[head])
            to_down = tn(bsp, ups[head])
            to_cross = tn(xsp, crs[head])
            up, cross, full, end = s["up"][...], s["cross"][...], s["full"][...], s["end"][...]
            q, k = s["q"][...], s["k"][...]
            rest = size - half
            d_q = from_same[:size] * up + to_full[:size] * full
            d_q = jnp.concatenate([d_q[:half], d_q[half:] + from_other[:rest] * cross[half:]], 0)
            d_k_up = from_same[size:] * up - (beta * to_full[size:]) * full
            d_k_up = jnp.concatenate(
                [d_k_up[:half], d_k_up[half:] + from_other[rest:] * cross[half:]], 0
            )
            k_end_part = d_ke * end
            d_k_down = to_down * s["down"][...] + k_end_part
            d_k_down = jnp.concatenate(
                [d_k_down[:half] + to_cross[:half] * cross[:half], d_k_down[half:]], 0
            )
            d_k = d_k_up + d_k_down
            d_cum = q * d_q + k * (d_k_up - d_k_down)
            end_state = fold(dot(ones8, tall(pack(state * cotan)), tb=True))[0:1, :]
            d_last = (
                jnp.sum(k * k_end_part, axis=0, keepdims=True)
                + dend_row[head, 0:1, :] * end_state
            )
            d_ld = ones_mm(upper, d_cum, 2) + d_last
            dgate_ref[:, cols] = s["slope"][...] * d_ld
            d_dlog = jnp.sum(s["ld"][...] * d_ld, axis=0, keepdims=True)
            d_braw = d_beta * (beta * (1.0 - beta))
            dbeta_ref[pl.ds(head, 1), :] = jnp.sum(
                jnp.where(r == c, d_braw, 0.0), axis=0, keepdims=True
            )
            d_q = s["qr"][...] * (d_q - q * jnp.sum(q * d_q, axis=1, keepdims=True))
            d_k = s["kr"][...] * (d_k - k * jnp.sum(k * d_k, axis=1, keepdims=True))
            red = []
            for j, (d_act, slope, out_ref) in enumerate(
                ((d_q, "sq", dq_ref), (d_k, "sk", dk_ref), (d_v, "sv", dv_ref))
            ):
                d_pre = d_act * s[slope][...]
                spot = dext.at[3 * g + j]
                spot[0:PAD, :] = jnp.zeros((PAD, width), F32)
                spot[PAD : PAD + size, :] = d_pre
                spot[PAD + size :, :] = jnp.zeros((PAD, width), F32)
                whole, tail = None, None
                for i in range(taps):
                    w = w_ref[j, i : i + 1, cols]
                    start = PAD + taps - 1 - i
                    term = w * spot[start : start + size, :]
                    edge = w * spot[taps - 1 - i : taps - 1 - i + PAD, :]
                    whole = term if whole is None else whole + term
                    tail = edge if tail is None else tail + edge
                    begin = PAD - taps + 1 + i
                    x = ext[head * 3 + j, begin : begin + size, :]
                    red.append(jnp.sum(d_pre * x, axis=0, keepdims=True))
                out_ref[:, cols] = whole.astype(BF16)
                tail_out[head, j * PAD : (j + 1) * PAD, :] = tail
                last_rows[head, j * LAST : (j + 1) * LAST, :] = whole[size - LAST :, :]
            red.append(d_dlog)
            red.append(jnp.zeros((RED - len(red), width), F32))
            red_level[level, head] = jnp.concatenate(red, 0)
        for other in other_levels:
            level_copy(b, level, other).start()

        @pl.when(me > 0)
        def _():
            tail_copy(b).start()

    def sum_levels(b):
        for other in other_levels:
            level_copy(b, other, other).wait_recv()
        spot = pl.ds(b * group, group)
        total = red_level[0, spot]
        for i in range(1, levels):
            total = total + red_level[i, spot]
        red_team[mine, spot] = total
        for other in others:
            team_copy(b, mine, other).start()

    order = [meet(own_block, i, blocks) for i in range(blocks)]
    for i in range(blocks):
        grads(order[i])
        if i:
            sum_levels(order[i - 1])
    sum_levels(order[-1])

    @pl.when(me == n - 1)
    def _():
        tail_in[...] = jnp.zeros_like(tail_in)

    for b in order:
        @pl.when(me < n - 1)
        def _():
            tail_copy(b).wait_recv()

    for head in range(heads):
        cols = slice(head * width, (head + 1) * width)
        for j, out_ref in enumerate((dq_ref, dk_ref, dv_ref)):
            rows = last_rows[head, j * LAST : (j + 1) * LAST, :]
            rows = jnp.concatenate(
                [rows[: LAST - PAD], rows[LAST - PAD :] + tail_in[head, j * PAD : (j + 1) * PAD, :]],
                0,
            )
            out_ref[size - LAST :, cols] = rows.astype(BF16)

    for b in order:
        for other in others:
            team_copy(b, other, other).wait_recv()
    for head in range(heads):
        cols = slice(head * width, (head + 1) * width)
        total = red_team[0, head]
        for i in range(1, team):
            total = total + red_team[i, head]
        for j in range(3):
            conv_ref[j, :, cols] = total[j * taps : (j + 1) * taps, :]
        decay_ref[:, cols] = total[3 * taps : 3 * taps + 1, :]

    for other in others:
        map_copy(mine, other).wait_send()
        off_copy(mine, other).wait_send()
        state_give(mine, other).wait_send()
        cotan_give(mine, other).wait_send()
        for b in order:
            team_copy(b, mine, other).wait_send()
    for other in other_levels:
        for b in order:
            level_copy(b, level, other).wait_send()

    @pl.when(me > 0)
    def _():
        for b in order:
            tail_copy(b).wait_send()

    @pl.when(level < levels - 1)
    def _():
        state_hop.wait_send()

    @pl.when(level > 0)
    def _():
        cotan_hop.wait_send()

    @pl.when(me < n - 1)
    def _():
        for j, ref in enumerate(raws):
            halo_copy(j, ref).wait_send()


def pack2(a, b):
    ah, al = split(a)
    bh, bl = split(b)
    return jnp.concatenate([ah, bh, al, bl], 1)


def write_kernel(count, *refs):
    sources, targets, spots = refs[:count], refs[count : 2 * count], refs[2 * count : 3 * count]
    sems = refs[-1]
    reads = [
        pltpu.make_async_copy(src, spot, sems.at[0, i])
        for i, (src, spot) in enumerate(zip(sources, spots))
    ]
    writes = [
        pltpu.make_async_copy(spot, dst, sems.at[1, i])
        for i, (spot, dst) in enumerate(zip(spots, targets))
    ]
    for copy in reads:
        copy.start()
    for i in range(count):
        reads[i].wait()
        writes[i].start()
    for copy in writes:
        copy.wait()


def per_device(query_raw, key_raw, value_raw, gate_raw, beta_raw, conv_weight, decay_log, grad_out):
    n = lax.axis_size("seq")
    size, channels = gate_raw.shape
    heads = beta_raw.shape[1]
    width = channels // heads
    group = GROUP if heads % GROUP == 0 else 1
    team = math.gcd(TEAM, math.gcd(n, heads))
    part = heads // team
    levels = n // team
    nblk = heads // group
    vmem = pl.BlockSpec(memory_space=pltpu.VMEM)
    hbm = pl.BlockSpec(memory_space=pltpu.HBM)
    act = jax.ShapeDtypeStruct((size, channels), BF16)
    shapes = (
        act, act, act,
        jax.ShapeDtypeStruct((size, channels), F32),
        jax.ShapeDtypeStruct((heads, size), F32),
        jax.ShapeDtypeStruct(conv_weight.shape, F32),
        jax.ShapeDtypeStruct((1, channels), F32),
    )

    def f32s(*shape):
        return pltpu.VMEM(shape, F32)

    def bf16s(*shape):
        return pltpu.VMEM(shape, BF16)

    def sems(*shape):
        return pltpu.SemaphoreType.DMA(shape)

    scratch = [
        pltpu.VMEM(query_raw.shape, query_raw.dtype), pltpu.VMEM(key_raw.shape, key_raw.dtype),
        pltpu.VMEM(value_raw.shape, value_raw.dtype), pltpu.VMEM(gate_raw.shape, F32),
        f32s(heads, size), pltpu.VMEM(conv_weight.shape, F32), f32s(1, channels),
        pltpu.VMEM(grad_out.shape, grad_out.dtype), sems(8),
        f32s(heads, len(NAMES), size, width),
        bf16s(heads, 2 * size, 2 * width), bf16s(heads, size, 2 * width),
        bf16s(heads, size, 2 * width), bf16s(heads, size, 2 * width),
        bf16s(heads, 2 * size, 2 * width), bf16s(heads, size, 2 * width),
        bf16s(heads, size, 2 * size), bf16s(heads, size, 2 * width),
        f32s(heads, 8, width),
        f32s(3 * heads, PAD + size, width), f32s(3 * group, PAD + size + PAD, width),
        pltpu.VMEM((3, PAD, channels), query_raw.dtype),
        bf16s(heads, width + 16, width), f32s(heads, 2 * width, width),
        bf16s(team, part, width + 16, width), f32s(team, part, 2 * width, width),
        f32s(team, part, width, width), f32s(team, part, width, width),
        f32s(heads, width, width), f32s(heads, width, width),
        f32s(part, width, width), f32s(part, width, width),
        f32s(part, width, width), f32s(part, width, width),
        f32s(levels, heads, RED, width), f32s(team, heads, RED, width),
        f32s(heads, 3 * PAD, width), f32s(heads, 3 * PAD, width),
        f32s(heads, 3 * LAST, width),
        sems(3), sems(3),
        sems(team), sems(team), sems(team), sems(team),
        sems(team), sems(team), sems(team), sems(team),
        pltpu.SemaphoreType.DMA, pltpu.SemaphoreType.DMA,
        pltpu.SemaphoreType.DMA, pltpu.SemaphoreType.DMA,
        sems(levels, nblk), sems(levels, nblk), sems(team, nblk), sems(team, nblk),
        sems(nblk), sems(nblk),
    ]
    results = pl.pallas_call(
        functools.partial(layer_kernel, group),
        out_shape=shapes,
        in_specs=[hbm] * 8,
        out_specs=(vmem,) * 7,
        scratch_shapes=scratch,
        compiler_params=pltpu.CompilerParams(
            collective_id=0, has_side_effects=True, vmem_limit_bytes=VMEM_LIMIT
        ),
        name="layer",
    )(
        query_raw, key_raw, value_raw, gate_raw, beta_raw.T, conv_weight,
        decay_log.reshape(1, channels), grad_out,
    )
    dq, dk, dv, dgate, dbeta, conv_sum, decay_sum = pl.pallas_call(
        functools.partial(write_kernel, len(shapes)),
        out_shape=shapes,
        in_specs=[hbm] * 7,
        out_specs=(hbm,) * 7,
        scratch_shapes=[pltpu.VMEM(x.shape, x.dtype) for x in shapes] + [sems(2, 7)],
        compiler_params=pltpu.CompilerParams(vmem_limit_bytes=VMEM_LIMIT),
        name="write",
    )(*results)
    return (dq, dk, dv, dgate, dbeta.T, conv_sum, decay_sum.reshape(channels))


def solution(mesh):
    in_specs = (
        P("seq", "head"),
        P("seq", "head"),
        P("seq", "head"),
        P("seq", "head"),
        P("seq", "head"),
        P(None, None, "head"),
        P("head"),
        P("seq", "head"),
    )
    out_specs = (
        P("seq", "head"),
        P("seq", "head"),
        P("seq", "head"),
        P("seq", "head"),
        P("seq", "head"),
        P(None, None, "head"),
        P("head"),
    )
    return jax.shard_map(
        per_device, mesh=mesh, in_specs=in_specs, out_specs=out_specs, check_vma=False
    )
```

time: 84.1 us -> 68.2 us (0.81)
  Pallas kernels: 80.1 us -> 67.2 us
  local copies, waits for them, and re-layouts: 2.06 us -> 0 us
  other arithmetic: 0.91 us -> 0 us
    pallas_call x3 -> x2, Pallas kernels: 80.1 us -> 67.2 us  [the longest x1 65 us: per_device(): pl.pallas_call(functools.partial(layer_kernel, group), out_shape=shapes,...]
    unnamed x8 -> x0, local copies, waits for them, and re-layouts: 1.44 us -> none
    convert_element_type x1 -> x0, other arithmetic: 0.91 us -> none  [per_device(): ends = (last + after).astype(BF16)]
where the time goes in v1:
time: 68.2 us; the launch traced here: 68 us
  Pallas kernels  67.2 us (99%)
  between operations  0.8 us (1%)
    pallas_call x1, Pallas kernels, per_device(): pl.pallas_call(functools.partial(layer_kernel, group), out_shape=shapes,...  65 us
    pallas_call x1, Pallas kernels, per_device(): pl.pallas_call(functools.partial(write_kernel, len(shapes)), out_shape=sh...  2.21 us

profile of v1, /device:TPU:0, one launch (start us, length us, event | category | flops | bytes accessed | tf_op | source)
XLA Modules:
  0.0 68.0 jit_solution(12605271216792417012)
XLA Ops:
  0.6 65.0 %layer.1 = (bf16[128,1024]{1,0:T(8,128)(2,1)}, bf16[128,1024]{1,0:T(8,128)(2,1)}, bf16[128,1024]{1,0:T(8,128)(2,1)}, f32[128,1024]{1,0:T(8,128)}, f32[8,128]{1,0...) custom-call(bf16[128,1024]{1,0:T(8,128)(2,1)} %q_hbm.1, bf16[128,1024]{1,0:T(8,128)(2,1)} %k_hbm.1, ...), custom_call_target="tpu_custom_call" | custom-call | tf_op jit(solution)/shard_map/layer/pallas_call | solution.py:807
  65.6 2.2 %write.1 = (bf16[128,1024]{1,0:T(8,128)(2,1)}, bf16[128,1024]{1,0:T(8,128)(2,1)}, bf16[128,1024]{1,0:T(8,128)(2,1)}, f32[128,1024]{1,0:T(8,128)}, f32[8,128]{1,0...) custom-call(bf16[128,1024]{1,0:T(8,128)(2,1)} %get-tuple-element.21.refs_0_, ...), custom_call_target="tpu_custom_call" | custom-call | tf_op jit(solution)/shard_map/write/pallas_call | solution.py:821

commit v2 on v1

--- a/solution.py
+++ b/solution.py
@@ -185,7 +185,8 @@
 def layer_kernel(
     group,
     q_hbm, k_hbm, v_hbm, gate_hbm, beta_hbm, w_hbm, dlog_hbm, grad_hbm,
-    dq_ref, dk_ref, dv_ref, dgate_ref, dbeta_ref, conv_ref, decay_ref,
+    dq_out, dk_out, dv_out, dgate_out, dbeta_out, conv_ref, decay_ref,
+    dq_ref, dk_ref, dv_ref, dgate_ref, dbeta_ref, store,
     q_ref, k_ref, v_ref, gate_ref, beta_ref, w_ref, dlog_ref, grad_ref, load,
     keep, wk, ki, kd, kc, ups, crs, inv_sp, ke_sp, dend_row,
     ext, dext, halo_in,
@@ -213,8 +214,8 @@
     loads = [
         pltpu.make_async_copy(src, dst, load.at[i])
         for i, (src, dst) in enumerate((
-            (q_hbm, q_ref), (k_hbm, k_ref), (v_hbm, v_ref), (gate_hbm, gate_ref),
-            (dlog_hbm, dlog_ref), (w_hbm, w_ref), (beta_hbm, beta_ref), (grad_hbm, grad_ref),
+            (dlog_hbm, dlog_ref), (gate_hbm, gate_ref), (q_hbm, q_ref), (k_hbm, k_ref),
+            (v_hbm, v_ref), (w_hbm, w_ref), (beta_hbm, beta_ref), (grad_hbm, grad_ref),
         ))
     ]
     for copy in loads:
@@ -225,10 +226,6 @@
     links += [right, left]
     for peer in links:
         pl.semaphore_signal(barrier, inc=1, device_id={"seq": peer}, device_id_type=mesh_id)
-    for copy in loads:
-        copy.wait()
-    pl.semaphore_wait(barrier, len(links))
-
     def remote(src, dst, send, recv, to):
         return pltpu.make_async_remote_copy(
             src_ref=src, dst_ref=dst, send_sem=send, recv_sem=recv,
@@ -242,11 +239,6 @@
 
     raws = (q_ref, k_ref, v_ref)
 
-    @pl.when(me < n - 1)
-    def _():
-        for j, ref in enumerate(raws):
-            halo_copy(j, ref).start()
-
     def block(member):
         return pl.ds(member * part, part)
 
@@ -259,11 +251,17 @@
             base + target,
         )
 
-    def off_copy(source, target):
+    def off_copy(slot, source, target):
         return remote(
-            off_out.at[block(target)], off_in.at[source], fs.at[target], fr.at[source],
-            base + target,
+            off_out.at[slot, block(target)], off_in.at[slot, source],
+            fs.at[slot, target], fr.at[slot, source], base + target,
         )
+
+    state_slot = 1
+    if levels > 1:
+        state_slot = level // (levels // 2)
+        if levels % 2:
+            state_slot = jnp.minimum(state_slot, 1)
 
     def state_give(owner, member):
         return remote(
@@ -288,6 +286,37 @@
     rr, cc = iotas(width)
     low = c < half
 
+    def block_at(step):
+        return meet(own_block, blocks - 1 - step, blocks)
+
+    def prepare(step):
+        for g in range(group):
+            slot = step * group + g
+            cols = lanes(block_at(step) * group + g)
+            s = saved(slot)
+            parts = decays(gate_ref[:, cols], dlog_ref[:, cols])
+            for name, value in zip(
+                ("ld", "slope", "up", "down", "cross", "full", "end"), parts
+            ):
+                s[name][...] = value
+            dend_row[slot] = jnp.broadcast_to(parts[-1], (8, width))
+
+    loads[0].wait()
+    loads[1].wait()
+    for step in range(blocks // 2):
+        prepare(step)
+    for copy in loads[2:]:
+        copy.wait()
+    pl.semaphore_wait(barrier, len(links))
+
+    @pl.when(me < n - 1)
+    def _():
+        for j, ref in enumerate(raws):
+            halo_copy(j, ref).start()
+
+    for step in range(blocks // 2, blocks):
+        prepare(step)
+
     @pl.when(me == 0)
     def _():
         halo_in[...] = jnp.zeros_like(halo_in)
@@ -297,19 +326,20 @@
         for j, ref in enumerate(raws):
             halo_copy(j, ref).wait_recv()
 
-    def maps(step):
-        start = meet(own_block, blocks - 1 - step, blocks) * group
+    def front(step):
+        start = block_at(step) * group
         held = []
         for g in range(group):
             head = start + g
+            slot = step * group + g
             cols = lanes(head)
-            s = saved(head)
-            ld, slope, up, down, cross, full, end, dend = decays(
-                gate_ref[:, cols], dlog_ref[:, cols]
-            )
+            s = saved(slot)
+            up, down, cross = s["up"][...], s["down"][...], s["cross"][...]
+            full, end = s["full"][...], s["end"][...]
+            dend = dend_row[slot, 0:1, :]
             acts = []
             for j, ref in enumerate(raws):
-                pre = conv_pre(ext.at[head * 3 + j], ref, halo_in, w_ref, j, cols)
+                pre = conv_pre(ext.at[slot * 3 + j], ref, halo_in, w_ref, j, cols)
                 sig = sigmoid(pre)
                 s[("sq", "sk", "sv")[j]][...] = sig * (1.0 + pre * (1.0 - sig))
                 acts.append(pre * sig)
@@ -318,23 +348,21 @@
             v = acts[2]
             beta = jnp.broadcast_to(sigmoid(pick_column(beta_ref, head)), (size, width))
             for name, value in (
-                ("q", q), ("k", k), ("v", v), ("up", up), ("down", down), ("cross", cross),
-                ("full", full), ("end", end), ("ld", ld), ("slope", slope), ("beta", beta),
+                ("q", q), ("k", k), ("v", v), ("beta", beta),
                 ("qr", jnp.broadcast_to(qr, (size, width))),
                 ("kr", jnp.broadcast_to(kr, (size, width))),
             ):
                 s[name][...] = value
-            dend_row[head] = jnp.broadcast_to(dend, (8, width))
             kfull = k * full
             ups_sp = pack(jnp.concatenate([q * up, k * up], 0))
-            ups[head] = ups_sp
+            ups[slot] = ups_sp
             kd_sp = pack(k * down)
-            kd[head] = kd_sp
+            kd[slot] = kd_sp
             kcross = k * cross
             kc_sp = pack(kcross)
-            kc[head] = kc_sp
+            kc[slot] = kc_sp
             crs_sp = pack(jnp.concatenate([(q * cross)[half:], kcross[half:]], 0))
-            crs[head] = crs_sp
+            crs[slot] = crs_sp
             same = nt(ups_sp, kd_sp)
             other = nt(crs_sp, kc_sp)
             rest = size - half
@@ -353,22 +381,26 @@
             both = dot(jnp.concatenate([ah, al], 1), grad, ta=True)
             reach = both[:size] + both[size:]
             s["reach"][...] = reach
-            wk[head, size:, :] = pack(kfull)
-            ke_sp[head] = pack(k * end)
+            wk[slot, size:, :] = pack(kfull)
+            ke_sp[slot] = pack(k * end)
             held.append((raw * beta, beta * kfull, beta * v, pack(q * full), reach, dend))
-        invs = unit_inverses([item[0] for item in held])
+        return held
+
+    def back(step, held, invs):
+        start = block_at(step) * group
         for g in range(group):
             head = start + g
+            slot = step * group + g
             cols = lanes(head)
-            s = saved(head)
+            s = saved(slot)
             isp = pack(invs[g])
-            inv_sp[head] = isp
+            inv_sp[slot] = isp
             by = nn(isp, pack2(held[g][1], held[g][2]))
             s["u"][...] = by[:, width:]
             bh, bl = split(by)
             wsp = jnp.concatenate([bh[:, :width], bl[:, :width]], 1)
-            wk[head, :size, :] = wsp
-            ends = tn(ke_sp[head], jnp.concatenate([bh, bl], 1))
+            wk[slot, :size, :] = wsp
+            ends = tn(ke_sp[slot], jnp.concatenate([bh, bl], 1))
             full_map = jnp.where(rr == cc, held[g][5], 0.0) - ends[:, :width]
             map_hi = full_map.astype(BF16)
             left_over = jnp.sum(
@@ -376,10 +408,10 @@
             )
             map_out[head, :width, :] = map_hi
             map_out[head, width:, :] = jnp.broadcast_to(left_over, (16, width)).astype(BF16)
-            off_out[head, :width, :] = ends[:, width:]
+            off_out[state_slot, head] = ends[:, width:]
             grad = grad_ref[:, cols]
             gsp = jnp.concatenate([grad, jnp.zeros_like(grad)], 1)
-            off_out[head, width:, :] = tn(
+            off_out[1 - state_slot, head] = tn(
                 jnp.concatenate([held[g][3], -wsp], 0),
                 jnp.concatenate([gsp, pack(held[g][4])], 0),
             )
@@ -390,34 +422,53 @@
             @pl.when((target != mine) & (lax.rem(head, part) == part - 1))
             def _():
                 map_copy(mine, target).start()
-                off_copy(mine, target).start()
-
+                off_copy(0, mine, target).start()
+
+    def send_rest(step):
+        start = block_at(step) * group
+        for g in range(group):
+            head = start + g
+            target = head // part
+
+            @pl.when((target != mine) & (lax.rem(head, part) == part - 1))
+            def _():
+                off_copy(1, mine, target).start()
+
+    held = front(0)
     for step in range(blocks):
-        maps(step)
+        invs = unit_inverses([item[0] for item in held])
+        later = front(step + 1) if step + 1 < blocks else None
+        back(step, held, invs)
+        held = later
+        if step:
+            send_rest(step - 1)
+    send_rest(blocks - 1)
     map_in[mine] = map_out[block(mine)]
-    off_in[mine] = off_out[block(mine)]
+    off_in[0, mine] = off_out[0, block(mine)]
+    off_in[1, mine] = off_out[1, block(mine)]
 
     def step_maps(j, h):
         both = map_in[j, h]
         rest = jnp.where(rr == cc, both[width : width + 1, :].astype(F32), 0.0).astype(BF16)
         return both[:width], rest
 
-    def forward_step(j, h, state):
+    def forward_step(slot, j, h, state):
         hi, rest = step_maps(j, h)
-        return nn(jnp.concatenate([hi, rest], 1), pack(state)) + off_in[j, h, :width, :]
-
-    def backward_step(j, h, cotan):
+        return nn(jnp.concatenate([hi, rest], 1), pack(state)) + off_in[slot, j, h]
+
+    def backward_step(slot, j, h, cotan):
         hi, rest = step_maps(j, h)
         out = fold(dot(jnp.concatenate([hi, rest], 0), twice(pack(cotan)), ta=True))
-        return out + off_in[j, h, width:, :]
-
-    def arrive(j):
+        return out + off_in[slot, j, h]
+
+    def arrive(slot, j):
         @pl.when(j != mine)
         def _():
-            map_copy(j, j).wait_recv()
-            off_copy(j, j).wait_recv()
-
-    def forward(first):
+            if slot == 0:
+                map_copy(j, j).wait_recv()
+            off_copy(slot, j, j).wait_recv()
+
+    def forward(slot):
         @pl.when(level == 0)
         def _():
             in_s[...] = jnp.zeros_like(in_s)
@@ -428,11 +479,10 @@
 
         states = [in_s[h] for h in range(part)]
         for j in range(team):
-            if first:
-                arrive(j)
+            arrive(slot, j)
             for h in range(part):
                 out_s[j, h] = states[h]
-                states[h] = forward_step(j, h, states[h])
+                states[h] = forward_step(slot, j, h, states[h])
 
         @pl.when(level < levels - 1)
         def _():
@@ -444,7 +494,7 @@
         for i in range(1, team):
             state_give(mine, meet(mine, i, team)).start()
 
-    def backward(first):
+    def backward(slot):
         @pl.when(level == levels - 1)
         def _():
             in_g[...] = jnp.zeros_like(in_g)
@@ -455,11 +505,10 @@
 
         cotans = [in_g[h] for h in range(part)]
         for j in range(team - 1, -1, -1):
-            if first:
-                arrive(j)
+            arrive(slot, j)
             for h in range(part):
                 out_g[j, h] = cotans[h]
-                cotans[h] = backward_step(j, h, cotans[h])
+                cotans[h] = backward_step(slot, j, h, cotans[h])
 
         @pl.when(level > 0)
         def _():
@@ -471,37 +520,34 @@
         for i in range(1, team):
             cotan_give(mine, meet(mine, i, team)).start()
 
-    def ready(head):
-        s = saved(head)
-        isp = inv_sp[head]
+    def ready(slot):
+        s = saved(slot)
+        isp = inv_sp[slot]
         rh, rl = split(s["reach"][...])
-        esp = ke_sp[head]
+        esp = ke_sp[slot]
         rhs = jnp.concatenate([rh, esp[:, :width], rl, esp[:, width:]], 1)
         out = tn(isp, rhs)
         s["reach"][...] = out[:, :width]
-        ki[head] = pack(out[:, width:])
-
-    for head in range(heads // 2):
-        ready(head)
+        ki[slot] = pack(out[:, width:])
 
     @pl.when(level < levels // 2)
     def _():
-        forward(True)
+        forward(0)
 
     @pl.when(level >= levels // 2)
     def _():
-        backward(True)
-
-    for head in range(heads // 2, heads):
-        ready(head)
+        backward(0)
+
+    for slot in range(heads):
+        ready(slot)
 
     @pl.when(level < levels // 2)
     def _():
-        backward(False)
+        backward(1)
 
     @pl.when(level >= levels // 2)
     def _():
-        forward(False)
+        forward(1)
 
     def level_copy(b, source, target):
         spot = red_level.at[source, pl.ds(b * group, group)]
@@ -523,7 +569,8 @@
     ones8 = jnp.ones((8, width), BF16)
     taps = w_ref.shape[1]
 
-    def grads(b):
+    def grads(i):
+        b = order[i]
         for g in range(group):
             head = b * group + g
             owner = head // part
@@ -535,14 +582,15 @@
 
         for g in range(group):
             head = b * group + g
+            slot = (blocks - 1 - i) * group + g
             cols = lanes(head)
-            s = saved(head)
+            s = saved(slot)
             state, cotan = state_in[head], cotan_in[head]
             ssp, csp = pack(state), pack(cotan)
-            wkx = nn(wk[head], ssp)
+            wkx = nn(wk[slot], ssp)
             deltas = s["u"][...] - wkx[:size]
             resid = s["v"][...] - wkx[size:]
-            d_err = s["reach"][...] + nn(ki[head], csp)
+            d_err = s["reach"][...] + nn(ki[slot], csp)
             beta = s["beta"][...]
             d_v = beta * d_err
             grad = grad_ref[:, cols]
@@ -572,10 +620,10 @@
                 0,
             )
             bsp, xsp = pack(both), pack(crossed)
-            from_same = nn(bsp, kd[head])
-            from_other = nn(xsp, kc[head])
-            to_down = tn(bsp, ups[head])
-            to_cross = tn(xsp, crs[head])
+            from_same = nn(bsp, kd[slot])
+            from_other = nn(xsp, kc[slot])
+            to_down = tn(bsp, ups[slot])
+            to_cross = tn(xsp, crs[slot])
             up, cross, full, end = s["up"][...], s["cross"][...], s["full"][...], s["end"][...]
             q, k = s["q"][...], s["k"][...]
             rest = size - half
@@ -595,7 +643,7 @@
             end_state = fold(dot(ones8, tall(pack(state * cotan)), tb=True))[0:1, :]
             d_last = (
                 jnp.sum(k * k_end_part, axis=0, keepdims=True)
-                + dend_row[head, 0:1, :] * end_state
+                + dend_row[slot, 0:1, :] * end_state
             )
             d_ld = ones_mm(upper, d_cum, 2) + d_last
             dgate_ref[:, cols] = s["slope"][...] * d_ld
@@ -607,28 +655,21 @@
             d_q = s["qr"][...] * (d_q - q * jnp.sum(q * d_q, axis=1, keepdims=True))
             d_k = s["kr"][...] * (d_k - k * jnp.sum(k * d_k, axis=1, keepdims=True))
             red = []
-            for j, (d_act, slope, out_ref) in enumerate(
-                ((d_q, "sq", dq_ref), (d_k, "sk", dk_ref), (d_v, "sv", dv_ref))
-            ):
+            for j, (d_act, slope) in enumerate(((d_q, "sq"), (d_k, "sk"), (d_v, "sv"))):
                 d_pre = d_act * s[slope][...]
-                spot = dext.at[3 * g + j]
+                spot = dext.at[3 * slot + j]
                 spot[0:PAD, :] = jnp.zeros((PAD, width), F32)
                 spot[PAD : PAD + size, :] = d_pre
                 spot[PAD + size :, :] = jnp.zeros((PAD, width), F32)
-                whole, tail = None, None
-                for i in range(taps):
-                    w = w_ref[j, i : i + 1, cols]
-                    start = PAD + taps - 1 - i
-                    term = w * spot[start : start + size, :]
-                    edge = w * spot[taps - 1 - i : taps - 1 - i + PAD, :]
-                    whole = term if whole is None else whole + term
+                tail = None
+                for tap in range(taps):
+                    w = w_ref[j, tap : tap + 1, cols]
+                    edge = w * spot[taps - 1 - tap : taps - 1 - tap + PAD, :]
                     tail = edge if tail is None else tail + edge
-                    begin = PAD - taps + 1 + i
-                    x = ext[head * 3 + j, begin : begin + size, :]
+                    begin = PAD - taps + 1 + tap
+                    x = ext[slot * 3 + j, begin : begin + size, :]
                     red.append(jnp.sum(d_pre * x, axis=0, keepdims=True))
-                out_ref[:, cols] = whole.astype(BF16)
                 tail_out[head, j * PAD : (j + 1) * PAD, :] = tail
-                last_rows[head, j * LAST : (j + 1) * LAST, :] = whole[size - LAST :, :]
             red.append(d_dlog)
             red.append(jnp.zeros((RED - len(red), width), F32))
             red_level[level, head] = jnp.concatenate(red, 0)
@@ -650,12 +691,41 @@
         for other in others:
             team_copy(b, mine, other).start()
 
+    def spread_back(i):
+        for g in range(group):
+            head = order[i] * group + g
+            slot = (blocks - 1 - i) * group + g
+            cols = lanes(head)
+            for j, out_ref in enumerate((dq_ref, dk_ref, dv_ref)):
+                spot = dext.at[3 * slot + j]
+                whole = None
+                for tap in range(taps):
+                    start = PAD + taps - 1 - tap
+                    term = w_ref[j, tap : tap + 1, cols] * spot[start : start + size, :]
+                    whole = term if whole is None else whole + term
+                out_ref[:, cols] = whole.astype(BF16)
+                last_rows[head, j * LAST : (j + 1) * LAST, :] = whole[size - LAST :, :]
+
     order = [meet(own_block, i, blocks) for i in range(blocks)]
     for i in range(blocks):
-        grads(order[i])
+        grads(i)
         if i:
             sum_levels(order[i - 1])
+    gate_write = pltpu.make_async_copy(dgate_ref, dgate_out, store.at[0])
+    beta_write = pltpu.make_async_copy(dbeta_ref, dbeta_out, store.at[1])
+    gate_write.start()
+    beta_write.start()
+    for i in range(blocks // 2):
+        spread_back(i)
     sum_levels(order[-1])
+    for i in range(blocks // 2, blocks):
+        spread_back(i)
+    bodies, ends = [], []
+    for j, (ref, out) in enumerate(((dq_ref, dq_out), (dk_ref, dk_out), (dv_ref, dv_out))):
+        top, bottom = pl.ds(0, size - LAST), pl.ds(size - LAST, LAST)
+        bodies.append(pltpu.make_async_copy(ref.at[top], out.at[top], store.at[2 + j]))
+        ends.append(pltpu.make_async_copy(ref.at[bottom], out.at[bottom], store.at[5 + j]))
+        bodies[-1].start()
 
     @pl.when(me == n - 1)
     def _():
@@ -675,6 +745,8 @@
                 0,
             )
             out_ref[size - LAST :, cols] = rows.astype(BF16)
+    for copy in ends:
+        copy.start()
 
     for b in order:
         for other in others:
@@ -688,9 +760,12 @@
             conv_ref[j, :, cols] = total[j * taps : (j + 1) * taps, :]
         decay_ref[:, cols] = total[3 * taps : 3 * taps + 1, :]
 
+    for copy in [gate_write, beta_write] + bodies + ends:
+        copy.wait()
     for other in others:
         map_copy(mine, other).wait_send()
-        off_copy(mine, other).wait_send()
+        off_copy(0, mine, other).wait_send()
+        off_copy(1, mine, other).wait_send()
         state_give(mine, other).wait_send()
         cotan_give(mine, other).wait_send()
         for b in order:
@@ -774,7 +849,8 @@
     def sems(*shape):
         return pltpu.SemaphoreType.DMA(shape)
 
-    scratch = [
+    scratch = [pltpu.VMEM(x.shape, x.dtype) for x in shapes[:5]] + [
+        sems(8),
         pltpu.VMEM(query_raw.shape, query_raw.dtype), pltpu.VMEM(key_raw.shape, key_raw.dtype),
         pltpu.VMEM(value_raw.shape, value_raw.dtype), pltpu.VMEM(gate_raw.shape, F32),
         f32s(heads, size), pltpu.VMEM(conv_weight.shape, F32), f32s(1, channels),
@@ -785,10 +861,10 @@
         bf16s(heads, 2 * size, 2 * width), bf16s(heads, size, 2 * width),
         bf16s(heads, size, 2 * size), bf16s(heads, size, 2 * width),
         f32s(heads, 8, width),
-        f32s(3 * heads, PAD + size, width), f32s(3 * group, PAD + size + PAD, width),
+        f32s(3 * heads, PAD + size, width), f32s(3 * heads, PAD + size + PAD, width),
         pltpu.VMEM((3, PAD, channels), query_raw.dtype),
-        bf16s(heads, width + 16, width), f32s(heads, 2 * width, width),
-        bf16s(team, part, width + 16, width), f32s(team, part, 2 * width, width),
+        bf16s(heads, width + 16, width), f32s(2, heads, width, width),
+        bf16s(team, part, width + 16, width), f32s(2, team, part, width, width),
         f32s(team, part, width, width), f32s(team, part, width, width),
         f32s(heads, width, width), f32s(heads, width, width),
         f32s(part, width, width), f32s(part, width, width),
@@ -797,7 +873,7 @@
         f32s(heads, 3 * PAD, width), f32s(heads, 3 * PAD, width),
         f32s(heads, 3 * LAST, width),
         sems(3), sems(3),
-        sems(team), sems(team), sems(team), sems(team),
+        sems(team), sems(team), sems(2, team), sems(2, team),
         sems(team), sems(team), sems(team), sems(team),
         pltpu.SemaphoreType.DMA, pltpu.SemaphoreType.DMA,
         pltpu.SemaphoreType.DMA, pltpu.SemaphoreType.DMA,
@@ -808,7 +884,7 @@
         functools.partial(layer_kernel, group),
         out_shape=shapes,
         in_specs=[hbm] * 8,
-        out_specs=(vmem,) * 7,
+        out_specs=(hbm,) * 5 + (vmem,) * 2,
         scratch_shapes=scratch,
         compiler_params=pltpu.CompilerParams(
             collective_id=0, has_side_effects=True, vmem_limit_bytes=VMEM_LIMIT

time: 68.2 us -> 64.1 us (0.940)
  Pallas kernels: 67.2 us -> 63.1 us
    pallas_call x1, Pallas kernels: 65 us -> 60.9 us  [per_device(): pl.pallas_call(functools.partial(layer_kernel, group), out_shape=shapes,...]
where the time goes in v2:
time: 64.1 us; the launch traced here: 63.9 us
  Pallas kernels  63.1 us (98%)
  between operations  0.8 us (1%)
    pallas_call x1, Pallas kernels, per_device(): pl.pallas_call(functools.partial(layer_kernel, group), out_shape=shapes,...  60.9 us
    pallas_call x1, Pallas kernels, per_device(): pl.pallas_call(functools.partial(write_kernel, len(shapes)), out_shape=sh...  2.21 us

profile of v2, /device:TPU:0, one launch (start us, length us, event | category | flops | bytes accessed | tf_op | source)
XLA Modules:
  0.0 63.9 jit_solution(920057631318887607)
XLA Ops:
  0.6 60.9 %layer.1 = (bf16[128,1024]{1,0:T(8,128)(2,1)}, bf16[128,1024]{1,0:T(8,128)(2,1)}, bf16[128,1024]{1,0:T(8,128)(2,1)}, f32[128,1024]{1,0:T(8,128)}, f32[8,128]{1,0...) custom-call(bf16[128,1024]{1,0:T(8,128)(2,1)} %q_hbm.1, bf16[128,1024]{1,0:T(8,128)(2,1)} %k_hbm.1, ...), custom_call_target="tpu_custom_call" | custom-call | tf_op jit(solution)/shard_map/layer/pallas_call | solution.py:883
  61.6 2.2 %write.1 = (bf16[128,1024]{1,0:T(8,128)(2,1)}, bf16[128,1024]{1,0:T(8,128)(2,1)}, bf16[128,1024]{1,0:T(8,128)(2,1)}, f32[128,1024]{1,0:T(8,128)}, f32[8,128]{1,0...) custom-call(bf16[128,1024]{1,0:T(8,128)(2,1)} %get-tuple-element.21.refs_0_, ...), custom_call_target="tpu_custom_call" | custom-call | tf_op jit(solution)/shard_map/write/pallas_call | solution.py:897

commit v3 on v2

--- a/solution.py
+++ b/solution.py
@@ -437,9 +437,8 @@
     held = front(0)
     for step in range(blocks):
         invs = unit_inverses([item[0] for item in held])
-        later = front(step + 1) if step + 1 < blocks else None
         back(step, held, invs)
-        held = later
+        held = front(step + 1) if step + 1 < blocks else None
         if step:
             send_rest(step - 1)
     send_rest(blocks - 1)

time: 64.1 us -> 62.6 us (0.977)
  Pallas kernels: 63.1 us -> 61.6 us
    pallas_call x1, Pallas kernels: 60.9 us -> 59.4 us  [per_device(): pl.pallas_call(functools.partial(layer_kernel, group), out_shape=shapes,...]
where the time goes in v3:
time: 62.6 us; the launch traced here: 62.4 us
  Pallas kernels  61.6 us (98%)
  between operations  0.8 us (1%)
    pallas_call x1, Pallas kernels, per_device(): pl.pallas_call(functools.partial(layer_kernel, group), out_shape=shapes,...  59.4 us
    pallas_call x1, Pallas kernels, per_device(): pl.pallas_call(functools.partial(write_kernel, len(shapes)), out_shape=sh...  2.21 us

profile of v3, /device:TPU:0, one launch (start us, length us, event | category | flops | bytes accessed | tf_op | source)
XLA Modules:
  0.0 62.4 jit_solution(7886205625491653785)
XLA Ops:
  0.6 59.4 %layer.1 = (bf16[128,1024]{1,0:T(8,128)(2,1)}, bf16[128,1024]{1,0:T(8,128)(2,1)}, bf16[128,1024]{1,0:T(8,128)(2,1)}, f32[128,1024]{1,0:T(8,128)}, f32[8,128]{1,0...) custom-call(bf16[128,1024]{1,0:T(8,128)(2,1)} %q_hbm.1, bf16[128,1024]{1,0:T(8,128)(2,1)} %k_hbm.1, ...), custom_call_target="tpu_custom_call" | custom-call | tf_op jit(solution)/shard_map/layer/pallas_call | solution.py:882
  60.0 2.2 %write.1 = (bf16[128,1024]{1,0:T(8,128)(2,1)}, bf16[128,1024]{1,0:T(8,128)(2,1)}, bf16[128,1024]{1,0:T(8,128)(2,1)}, f32[128,1024]{1,0:T(8,128)}, f32[8,128]{1,0...) custom-call(bf16[128,1024]{1,0:T(8,128)(2,1)} %get-tuple-element.21.refs_0_, ...), custom_call_target="tpu_custom_call" | custom-call | tf_op jit(solution)/shard_map/write/pallas_call | solution.py:896

commit v4 on v3

--- a/solution.py
+++ b/solution.py
@@ -714,10 +714,8 @@
     beta_write = pltpu.make_async_copy(dbeta_ref, dbeta_out, store.at[1])
     gate_write.start()
     beta_write.start()
-    for i in range(blocks // 2):
-        spread_back(i)
     sum_levels(order[-1])
-    for i in range(blocks // 2, blocks):
+    for i in range(blocks):
         spread_back(i)
     bodies, ends = [], []
     for j, (ref, out) in enumerate(((dq_ref, dq_out), (dk_ref, dk_out), (dv_ref, dv_out))):

time: 62.6 us -> 62.6 us (level)
  no operation moved by 1% of the time
where the time goes in v4:
time: 62.6 us; the launch traced here: 62.4 us
  Pallas kernels  61.6 us (98%)
  between operations  0.8 us (1%)
    pallas_call x1, Pallas kernels, per_device(): pl.pallas_call(functools.partial(layer_kernel, group), out_shape=shapes,...  59.4 us
    pallas_call x1, Pallas kernels, per_device(): pl.pallas_call(functools.partial(write_kernel, len(shapes)), out_shape=sh...  2.21 us

profile of v4, /device:TPU:0, one launch (start us, length us, event | category | flops | bytes accessed | tf_op | source)
XLA Modules:
  0.0 62.4 jit_solution(10560093203395187639)
XLA Ops:
  0.6 59.4 %layer.1 = (bf16[128,1024]{1,0:T(8,128)(2,1)}, bf16[128,1024]{1,0:T(8,128)(2,1)}, bf16[128,1024]{1,0:T(8,128)(2,1)}, f32[128,1024]{1,0:T(8,128)}, f32[8,128]{1,0...) custom-call(bf16[128,1024]{1,0:T(8,128)(2,1)} %q_hbm.1, bf16[128,1024]{1,0:T(8,128)(2,1)} %k_hbm.1, ...), custom_call_target="tpu_custom_call" | custom-call | tf_op jit(solution)/shard_map/layer/pallas_call | solution.py:880
  60.0 2.2 %write.1 = (bf16[128,1024]{1,0:T(8,128)(2,1)}, bf16[128,1024]{1,0:T(8,128)(2,1)}, bf16[128,1024]{1,0:T(8,128)(2,1)}, f32[128,1024]{1,0:T(8,128)}, f32[8,128]{1,0...) custom-call(bf16[128,1024]{1,0:T(8,128)(2,1)} %get-tuple-element.21.refs_0_, ...), custom_call_target="tpu_custom_call" | custom-call | tf_op jit(solution)/shard_map/write/pallas_call | solution.py:894
